TPU v7x, 128 devices: a whole 4x4x4 slice. The times are simulated.
128 devices in a mesh: row: 16 (over x, z), col: 8 (over y, core).
Axes of the slice: x: 4, y: 4, z: 4, core: 2. Of those that a mesh axis runs over, the one named last changes fastest.
Arguments:
- child_tiles: float32 [1024, 256, 256], P(('row', 'col')), may hold values from -2 to 2
- tile_dest: int32 [1024, 2], P(('row', 'col')), may hold values from 0 to 31, as said below
- tile_counts: int32 [16, 8], P('row', 'col'), may hold values from 4 to 8
- child_offsets: int32 [4], replicated, may hold values from 0 to 16
Outputs:
- r_top: float32 [1024, 8192], P(None, 'col')
Inputs may be any that keep to these rules, and one draw needn't show every extreme that they name: tile_dest[t, 0] is a column tile of the front and tile_dest[t, 1] is below 7. Among the 8 slots of one count entry, at most 2 name column tiles of one block of 4 consecutive column tiles (blocks start at multiples of 4); some entry reaches 2 for some block, and some block receives 2 live slots from every entry that shares a row offset residue.
All inputs are finite; a program needn't handle non-finite values.
Results may differ from a plain program's by a relative error of at most 0.00008.
Values sent between devices are 32-bit elements; how exact they have to be, the bound alone decides.
No kernel may reach another device: no remote copies, remote signals or barrier semaphores. Data moves between devices by JAX's collectives and lax.ppermute only.
A program may use at most 128 MiB of HBM per device.

v0:
```python
import jax
import jax.numpy as jnp
from jax import lax
from jax.sharding import PartitionSpec as P

NC = 8192
PANELS = 4
CHILDREN = 4
CAPC = 2
ROT_BITS = 4
RTD = 8


def shifted(value, axis, by):
    count = lax.axis_size(axis)
    return lax.ppermute(value, axis, [(i, (i + by) % count) for i in range(count)])


def padded_to(lines, count):
    spare = -lines.shape[0] % count
    if not spare:
        return lines
    return jnp.concatenate([lines, jnp.zeros((spare, *lines.shape[1:]), lines.dtype)])


def from_root(value, axis, root):
    lines = jnp.where(lax.axis_index(axis) == root, value, jnp.zeros_like(value)).reshape(
        -1, *value.shape[1:][-1:]
    )
    padded = padded_to(lines, lax.axis_size(axis))
    own = lax.psum_scatter(padded, axis, scatter_dimension=0, tiled=True)
    return lax.all_gather(own, axis, axis=0, tiled=True)[: len(lines)].reshape(value.shape)


def shards(child_tiles, tile_dest, tile_counts, child_offsets):
    row_count = lax.axis_size("row")
    col_count = lax.axis_size("col")
    row_here = lax.axis_index("row")
    col_here = lax.axis_index("col")
    slot_count = child_tiles.shape[0]
    tile_size = child_tiles.shape[1]
    cols_local = NC // col_count
    tiles_col = cols_local // tile_size
    highest = lax.Precision.HIGHEST
    count_here = tile_counts[0, 0]
    slot_ids = jnp.arange(slot_count, dtype=jnp.int32)
    live_mask = slot_ids < count_here
    child_here = col_here // (col_count // CHILDREN)
    offset_here = jnp.sum(jnp.where(jnp.arange(CHILDREN) == child_here, child_offsets, 0))
    owner_col = tile_dest[:, 0] // tiles_col
    local_col = tile_dest[:, 0] % tiles_col
    local_row = tile_dest[:, 1] + (offset_here + row_here) // row_count
    position = local_row * tiles_col + local_col
    owner_dest = jnp.where(live_mask, owner_col, -1)
    metadata = jnp.stack([owner_dest, position], axis=1)
    amount = offset_here % row_count
    moved_tiles = child_tiles
    moved_meta = metadata
    for bit_index in range(ROT_BITS):
        shifted_tiles, shifted_meta = shifted((moved_tiles, moved_meta), "row", 1 << bit_index)
        take_bit = amount >> bit_index & 1 == 1
        moved_tiles = jnp.where(take_bit, shifted_tiles, moved_tiles)
        moved_meta = jnp.where(take_bit, shifted_meta, moved_meta)
    owner_ids = moved_meta[:, 0]
    owner_hits = (owner_ids[:, None] == jnp.arange(col_count)[None, :]).astype(jnp.int32)
    owner_rank = jnp.sum((jnp.cumsum(owner_hits, axis=0) - 1) * owner_hits, axis=1)
    bucket_id = jnp.where(owner_ids >= 0, owner_ids * CAPC + owner_rank, -1)
    picker = (jnp.arange(col_count * CAPC)[:, None] == bucket_id[None, :]).astype(jnp.float32)
    packed = jnp.einsum("bs,sxy->bxy", picker, moved_tiles, precision=highest)
    filled = jnp.sum(picker, axis=1)
    chosen_pos = jnp.sum(jnp.where(picker > 0, moved_meta[None, :, 1], 0), axis=1)
    packed_pos = jnp.where(filled > 0, chosen_pos, -1).astype(jnp.int32)
    packed = packed.reshape(col_count, CAPC, tile_size, tile_size)
    packed_pos = packed_pos.reshape(col_count, CAPC)
    arrived, arrived_pos = (
        lax.all_to_all(packed, "col", split_axis=0, concat_axis=0, tiled=True),
        lax.all_to_all(packed_pos, "col", split_axis=0, concat_axis=0, tiled=True),
    )
    arrived = arrived.reshape(col_count * CAPC, tile_size, tile_size)
    arrived_pos = arrived_pos.reshape(col_count * CAPC)
    placer = (arrived_pos[:, None] == jnp.arange(RTD * tiles_col)[None, :]).astype(jnp.float32)
    placer = placer.reshape(col_count * CAPC, RTD, tiles_col)
    front_local = jnp.einsum("brc,bxy->rxcy", placer, arrived, precision=highest)
    front_local = front_local.reshape(RTD * tile_size, cols_local)
    width = PANELS * tile_size
    col_index = col_here * cols_local + jnp.arange(cols_local)
    leading = from_root(front_local, "col", 0)
    gram_block = jnp.einsum("ri,rj->ij", leading, leading, precision=highest)
    cross_terms = jnp.einsum("ri,rj->ij", leading, front_local, precision=highest)
    gram_block, cross_terms = lax.psum((gram_block, cross_terms), "row")
    lower_factor = jnp.linalg.cholesky(gram_block)
    rows_out = jax.scipy.linalg.solve_triangular(lower_factor, cross_terms, lower=True)
    row_index = jnp.arange(width)
    result = jnp.where(col_index[None, :] >= row_index[:, None], rows_out, jnp.zeros_like(rows_out))
    return result


def solution(mesh):
    return jax.shard_map(
        shards,
        mesh=mesh,
        in_specs=(P(("row", "col"), None, None), P(("row", "col"), None), P("row", "col"), P()),
        out_specs=P(None, "col"),
        check_vma=False,
    )
```

profile of v0, /device:TPU:1, one launch (start us, length us, event | category | flops | bytes accessed | tf_op | source)
XLA Modules:
  0.0 1001.6 jit_solution(12923739866905033209)
XLA Ops:
  12.2 46.8 %collective-permute-done.4 = f32[8,256,256]{2,1,0:T(8,128)} collective-permute-done((f32[8,256,256]{2,1,0:T(8,128)}, f32[8,256,256]{2,1,0:T(8,128)}, u32[]{:S(2)}, u32[]{:S(2)}) %collective-permute-start.4) | collective-permute-done | bytes 2097184 | tf_op jit(solution)/shard_map/ppermute | solution.py:16
  62.3 48.4 %collective-permute-done.5 = f32[8,256,256]{2,1,0:T(8,128)} collective-permute-done((f32[8,256,256]{2,1,0:T(8,128)S(1)}, f32[8,256,256]{2,1,0:T(8,128)}, u32[]{:S(2)}, u32[]{:S(2)}) %collective-permute-start.5) | collective-permute-done | bytes 2097184 | tf_op jit(solution)/shard_map/ppermute | solution.py:16
  114.1 44.8 %collective-permute-done.6 = f32[8,256,256]{2,1,0:T(8,128)} collective-permute-done((f32[8,256,256]{2,1,0:T(8,128)S(1)}, f32[8,256,256]{2,1,0:T(8,128)}, u32[]{:S(2)}, u32[]{:S(2)}) %collective-permute-start.6) | collective-permute-done | bytes 2097184 | tf_op jit(solution)/shard_map/ppermute | solution.py:16
  167.2 36.4 %collective-permute-start.2 = (s32[8,2]{0,1:T(2,128)S(1)}, s32[8,2]{0,1:T(2,128)S(1)}, u32[]{:S(2)}, u32[]{:S(2)}) collective-permute-start(s32[8,2]{0,1:T(2,128)S(1)} %broadcast_select_fusion.6), channel_id=1, source_target_pairs={{0,32},{8,40},{16,48},{24,56},{32,64},{40,72},{48,80},{56,88},{64,... | collective-permute-start | bytes 200 | tf_op jit(solution)/shard_map/ppermute | solution.py:16
  211.7 10.0 all-to-all-start.1
  243.8 47.4 %all-to-all-done = f32[8,2,256,256]{3,1,2,0:T(2,128)} async-done(((f32[8,2,256,256]{3,1,2,0:T(2,128)}), f32[8,2,256,256]{3,1,2,0:T(2,128)}, u32[]{:S(2)}, u32[]{:S(2)}) %all-to-all-start) | async-done | bytes 4194336 | tf_op jit(solution)/shard_map/all_to_all | solution.py:76
  312.4 10.4 %copy.23 = f32[8,256,4,256]{1,0,3,2:T(8,128)} copy(f32[8,256,4,256]{3,0,2,1:T(8,128)} %fusion.4) | data formatting | bytes 16777216 | tf_op jit(solution)/shard_map/brc,bxy->rxcy/transpose | solution.py:83
  337.7 48.0 %reduce-scatter.2.cloned.1.call-done = f32[256,1024]{0,1:T(8,128)} async-done(((f32[2048,1024]{0,1:T(8,128)}), f32[256,1024]{0,1:T(8,128)}) %reduce-scatter.2.cloned.1.call-update) | async-done | bytes 1048592 | tf_op jit(solution)/shard_map/reduce_scatter | solution.py:31
  386.3 51.4 %all-gather.2.cloned.1.call-done = f32[2048,1024]{0,1:T(8,128)} async-done(((f32[256,1024]{0,1:T(8,128)}), f32[2048,1024]{0,1:T(8,128)}) %all-gather.2.cloned.1.call-update) | async-done | bytes 8388624 | tf_op jit(solution)/shard_map/all_gather | solution.py:32
  437.7 32.7 %fusion.88 = f32[1024,1024]{0,1:T(8,128)} fusion(f32[2048,1024]{0,1:T(8,128)} %all-gather.2.cloned.1.call-done), kind=kOutput, calls=%fused_computation.202 | convolution fusion | flops 25769803776 | bytes 12582912 | tf_op jit(solution)/shard_map/ri,rj->ij/dot_general | solution.py:88
  470.4 35.5 %fusion.89 = f32[1024,1024]{1,0:T(8,128)} fusion(f32[2048,1024]{0,1:T(8,128)S(1)} %copy-done.6, f32[2048,1024]{0,1:T(8,128)} %bitcast.137), kind=kOutput, calls=%fused_computation.203 | convolution fusion | flops 25769803776 | bytes 20971520 | tf_op jit(solution)/shard_map/ri,rj->ij/dot_general | solution.py:89
  506.0 141.6 %all-reduce.4.cloned.1.call-done = (f32[1024,1024]{1,0:T(8,128)}, f32[1024,1024]{0,1:T(8,128)}) async-done(((f32[1024,1024]{1,0:T(8,128)}, f32[1024,1024]{0,1:T(8,128)}), (f32[1024,1024]{1,0:T(8,128)}, f32[1024,1024]{0,1:T(8,128)})) %all-reduce.4.cloned.1.call-update) | async-done | bytes 8388624 | tf_op jit(solution)/shard_map/psum | solution.py:90
  659.5 11.7 %cholesky.223 = f32[128,128]{1,0:T(8,128)S(1)} custom-call(f32[128,128]{1,0:T(8,128)S(1)} %cholesky.580), custom_call_target="Cholesky" | custom-call | tf_op jit(solution)/shard_map/jit(cholesky)/cholesky | solution.py:91
  687.5 11.9 %cholesky.244 = f32[128,128]{1,0:T(8,128)S(1)} custom-call(f32[128,128]{1,0:T(8,128)S(1)} %cholesky.584), custom_call_target="Cholesky" | custom-call | tf_op jit(solution)/shard_map/jit(cholesky)/cholesky | solution.py:91
  713.2 11.7 %cholesky.468 = f32[128,128]{1,0:T(8,128)S(1)} custom-call(f32[128,128]{1,0:T(8,128)S(1)} %cholesky.589), custom_call_target="Cholesky" | custom-call | tf_op jit(solution)/shard_map/jit(cholesky)/cholesky | solution.py:91
  726.1 9.8 custom-call.65
  739.4 12.1 %cholesky.487 = f32[128,128]{1,0:T(8,128)S(1)} custom-call(f32[128,128]{1,0:T(8,128)S(1)} %cholesky.594), custom_call_target="Cholesky" | custom-call | tf_op jit(solution)/shard_map/jit(cholesky)/cholesky | solution.py:91
  766.0 11.7 %cholesky.506 = f32[128,128]{1,0:T(8,128)S(1)} custom-call(f32[128,128]{1,0:T(8,128)S(1)} %cholesky.599), custom_call_target="Cholesky" | custom-call | tf_op jit(solution)/shard_map/jit(cholesky)/cholesky | solution.py:91
  779.0 10.0 custom-call.67
  792.3 11.7 %cholesky.526 = f32[128,128]{1,0:T(8,128)S(1)} custom-call(f32[128,128]{1,0:T(8,128)S(1)} %cholesky.604), custom_call_target="Cholesky" | custom-call | tf_op jit(solution)/shard_map/jit(cholesky)/cholesky | solution.py:91
  818.1 11.9 %cholesky.546 = f32[128,128]{1,0:T(8,128)S(1)} custom-call(f32[128,128]{1,0:T(8,128)S(1)} %cholesky.609), custom_call_target="Cholesky" | custom-call | tf_op jit(solution)/shard_map/jit(cholesky)/cholesky | solution.py:91
  843.7 11.7 %cholesky.564 = f32[128,128]{1,0:T(8,128)S(1)} custom-call(f32[128,128]{1,0:T(8,128)S(1)} %convolution_subtract_fusion.11), custom_call_target="Cholesky" | custom-call | tf_op jit(solution)/shard_map/jit(cholesky)/cholesky | solution.py:91
  867.1 22.8 %while.1 = (s32[]{:T(128)}, f32[1024,1024]{1,0:T(8,128)}, s32[8,2]{0,1:T(2,128)S(1)}, f32[8,128,128]{2,1,0:T(8,128)S(1)}, s32[]{:T(128)}) while((s32[]{:T(128)}, f32[1024,1024]{1,0:T(8,128)}, s32[8,2]{0,1:T(2,128)S(1)}, f32[8,128,128]{2,1,0:T(8,128)S(1)}, s32[]{:T(128)}) %tuple.59), condition=%wide.while_cond, body=%wide.while_body.sunk | while | flops 2 | bytes 131181 | solution.py:92
  890.0 79.0 %custom-call.70 = f32[8,128,128]{1,2,0:T(8,128)S(1)} custom-call(f32[8,128,128]{2,1,0:T(8,128)S(1)} %get-tuple-element.12), custom_call_target="InvertDiagBlocksLowerTriangular" | custom-call | tf_op jit(solution)/shard_map/jit(_solve_triangular)/triangular_solve | solution.py:92
  (155 shorter events, 232.9 us)
Async XLA Ops:
  6.5 52.5 %collective-permute-start.4 = (f32[8,256,256]{2,1,0:T(8,128)}, f32[8,256,256]{2,1,0:T(8,128)}, u32[]{:S(2)}, u32[]{:S(2)}) collective-permute-start(f32[8,256,256]{2,1,0:T(8,128)} %param.4), channel_id=1, source_target_pairs={{0,8},{8,16},{16,24},{24,32},{32,40},{40,48},{48,56},{56,64},{64,7... | collective-permute-start | bytes 6291464 | tf_op jit(solution)/shard_map/ppermute | solution.py:16
  60.9 1.3 copy-start.3
  60.9 53.0 %copy-start.5 = (s32[8,2]{0,1:T(2,128)S(1)}, s32[8,2]{0,1:T(2,128)}, u32[]{:S(2)}) copy-start(s32[8,2]{0,1:T(2,128)} %param.5) | copy-start | bytes 196
  61.0 49.7 %collective-permute-start.5 = (f32[8,256,256]{2,1,0:T(8,128)S(1)}, f32[8,256,256]{2,1,0:T(8,128)}, u32[]{:S(2)}, u32[]{:S(2)}) collective-permute-start(f32[8,256,256]{2,1,0:T(8,128)S(1)} %broadcast_select_fusion.1), channel_id=1, source_target_pairs={{0,16},{8,24},{16,32},{24,40},{32,48},{40,56},{48,64},{56,72},{64,... | collective-permute-start | bytes 6291464 | tf_op jit(solution)/shard_map/ppermute | solution.py:16
  112.6 1.5 copy-start.2
  112.6 46.4 %collective-permute-start.6 = (f32[8,256,256]{2,1,0:T(8,128)S(1)}, f32[8,256,256]{2,1,0:T(8,128)}, u32[]{:S(2)}, u32[]{:S(2)}) collective-permute-start(f32[8,256,256]{2,1,0:T(8,128)S(1)} %broadcast_select_fusion.2), channel_id=1, source_target_pairs={{0,32},{8,40},{16,48},{24,56},{32,64},{40,72},{48,80},{56,88},{64,... | collective-permute-start | bytes 6291464 | tf_op jit(solution)/shard_map/ppermute | solution.py:16
  114.0 47.0 %collective-permute-start = (s32[8,2]{0,1:T(2,128)S(1)}, s32[8,2]{0,1:T(2,128)S(1)}, u32[]{:S(2)}, u32[]{:S(2)}) collective-permute-start(s32[8,2]{0,1:T(2,128)S(1)} %pad_add_fusion), channel_id=1, source_target_pairs={{0,8},{8,16},{16,24},{24,32},{32,40},{40,48},{48,56},{56,64},{64,7... | collective-permute-start | bytes 200 | tf_op jit(solution)/shard_map/ppermute | solution.py:16
  160.9 60.8 %collective-permute-start.7 = (f32[8,256,256]{2,1,0:T(8,128)S(1)}, f32[8,256,256]{2,1,0:T(8,128)}, u32[]{:S(2)}, u32[]{:S(2)}) collective-permute-start(f32[8,256,256]{2,1,0:T(8,128)S(1)} %broadcast_select_fusion.3), channel_id=1, source_target_pairs={{0,64},{8,72},{16,80},{24,88},{32,96},{40,104},{48,112},{56,120},{... | collective-permute-start | bytes 6291464 | tf_op jit(solution)/shard_map/ppermute | solution.py:16
  161.0 6.2 collective-permute-start.1
  167.2 39.3 %collective-permute-start.2 = (s32[8,2]{0,1:T(2,128)S(1)}, s32[8,2]{0,1:T(2,128)S(1)}, u32[]{:S(2)}, u32[]{:S(2)}) collective-permute-start(s32[8,2]{0,1:T(2,128)S(1)} %broadcast_select_fusion.6), channel_id=1, source_target_pairs={{0,32},{8,40},{16,48},{24,56},{32,64},{40,72},{48,80},{56,88},{64,... | collective-permute-start | bytes 200 | tf_op jit(solution)/shard_map/ppermute | solution.py:16
  206.6 3.9 collective-permute-start.3
  211.7 25.8 %all-to-all-start.1 = ((s32[8,1,2]{2,1,0:T(1,128)}), s32[8,1,2]{2,1,0:T(1,128)S(1)}, u32[]{:S(2)}, u32[]{:S(2)}) async-start(s32[8,1,2]{2,1,0:T(1,128)} %bitcast.5), calls=%async_computation.1 | async-start | bytes 8192 | tf_op jit(solution)/shard_map/all_to_all | solution.py:77
  237.5 53.7 %all-to-all-start = ((f32[8,2,256,256]{3,1,2,0:T(2,128)}), f32[8,2,256,256]{3,1,2,0:T(2,128)}, u32[]{:S(2)}, u32[]{:S(2)}) async-start(f32[8,2,256,256]{3,1,2,0:T(2,128)} %copy.20), calls=%async_computation | async-start | bytes 8388608 | tf_op jit(solution)/shard_map/all_to_all | solution.py:76
  242.3 143.4 %reduce-scatter.2.cloned.1.call-start = ((), (), s32[]{:S(2)}) async-start(), calls=%async_computation.3 | async-start | bytes 9437184 | tf_op jit(solution)/shard_map/reduce_scatter | solution.py:31
  330.3 3.2 copy-start
  337.6 100.1 %all-gather.2.cloned.1.call-start = ((), (), s32[]{:S(2)}) async-start(), calls=%async_computation.4 | async-start | bytes 9437184 | tf_op jit(solution)/shard_map/all_gather | solution.py:32
  385.7 261.9 %all-reduce.4.cloned.1.call-start = ((), (), s32[]{:S(2)}) async-start(), calls=%async_computation.5 | async-start | bytes 16777216 | tf_op jit(solution)/shard_map/psum | solution.py:90
  437.7 32.7 %copy-start.6 = (f32[2048,1024]{0,1:T(8,128)S(1)}, f32[2048,1024]{0,1:T(8,128)}, u32[]{:S(2)}) copy-start(f32[2048,1024]{0,1:T(8,128)} %all-gather.2.cloned.1.call-done) | copy-start | bytes 25165828
  657.5 2.0 copy-start.1
  969.0 4.3 copy-start.4
Sparse Core Ops, SparseCore 0:
  337.7 47.9 reduce-scatter.1
  387.4 50.2 all-gather.1
  506.1 141.4 all-reduce.3
where the time goes:
time: 1010 us; the launch traced here: 1000 us
  waiting for transfers between devices  441 us (44%)
  other arithmetic  276 us (27%)
  matrix products  127 us (13%)
  local copies, waits for them, and re-layouts  80.6 us (8%)
  starting transfers between devices  55.3 us (5%)
  between operations  21.9 us (2%)
    another operation x30, other arithmetic, shards(): lower_factor = jnp.linalg.cholesky(gram_block)  172 us
    ppermute x8, waiting for transfers between devices, shifted(): lax.ppermute(value, axis, [(i, (i + by) % count) for i in range(count)])  153 us
    psum x1, waiting for transfers between devices, shards(): gram_block, cross_terms = lax.psum((gram_block, cross_terms), 'row')  142 us
    another operation x3, other arithmetic, shards(): jax.scipy.linalg.solve_triangular(lower_factor, cross_terms, lower=True)  83.9 us
    all_gather x1, waiting for transfers between devices, from_root(): lax.all_gather(own, axis, axis=0, tiled=True)[:len(lines)]  51.4 us
    reduce_scatter x1, waiting for transfers between devices, from_root(): own = lax.psum_scatter(padded, axis, scatter_dimension=0, tiled=True)  48 us
    all_to_all x1, waiting for transfers between devices, shards(): lax.all_to_all(packed, 'col', split_axis=0, concat_axis=0, tiled=True)  47.4 us
    ppermute x8, starting transfers between devices, shifted(): lax.ppermute(value, axis, [(i, (i + by) % count) for i in range(count)])  39.7 us
  transfers between devices with their start and end apart: 13, of which 10 were waited for; matrix products, arithmetic and copies ran while one was open for 2% of the time, Pallas kernels for 0%

commit v1 on v0

--- a/solution.py
+++ b/solution.py
@@ -29,7 +29,9 @@
     )
     padded = padded_to(lines, lax.axis_size(axis))
     own = lax.psum_scatter(padded, axis, scatter_dimension=0, tiled=True)
-    return lax.all_gather(own, axis, axis=0, tiled=True)[: len(lines)].reshape(value.shape)
+    return jnp.concatenate(
+        lax.all_to_all(jnp.stack([own] * lax.axis_size(axis)), axis, 0, 0), axis=0
+    )[: len(lines)].reshape(value.shape)
 
 
 def shards(child_tiles, tile_dest, tile_counts, child_offsets):

time: 1010 us -> 1080 us (1.069)
  blocking collectives: 0 us -> 99 us
  waiting for transfers between devices: 441 us -> 390 us
  matrix products: 127 us -> 143 us
    all_to_all x0 -> x1, blocking collectives: none -> 99 us  [from_root(): lax.all_to_all(jnp.stack([own] * lax.axis_size(axis)), axis, 0, 0)]
    all_gather x1 -> x0, waiting for transfers between devices: 51.4 us -> none  [from_root(): lax.all_gather(own, axis, axis=0, tiled=True)[:len(lines)]]
    dot_general x1, matrix products: 35.5 us -> 55.4 us  [shards(): jnp.einsum('ri,rj->ij', leading, front_local, precision=highest)]
    another operation x24 -> x25, local copies, waits for them, and re-layouts: 22.7 us -> 23.8 us
  transfers between devices with their start and end apart: 13 -> 12, of which waited for: 10 -> 9; matrix products, arithmetic and copies ran while one was open for 2% -> 2% of each run, Pallas kernels for 0% -> 0%
where the time goes in v1:
time: 1080 us; the launch traced here: 1070 us
  waiting for transfers between devices  390 us (36%)
  other arithmetic  276 us (26%)
  matrix products  143 us (13%)
  blocking collectives  99 us (9%)
  local copies, waits for them, and re-layouts  83.1 us (8%)
  starting transfers between devices  54.7 us (5%)
  between operations  22.3 us (2%)
    another operation x30, other arithmetic, shards(): lower_factor = jnp.linalg.cholesky(gram_block)  172 us
    ppermute x8, waiting for transfers between devices, shifted(): lax.ppermute(value, axis, [(i, (i + by) % count) for i in range(count)])  153 us
    psum x1, waiting for transfers between devices, shards(): gram_block, cross_terms = lax.psum((gram_block, cross_terms), 'row')  142 us
    all_to_all x1, blocking collectives, from_root(): lax.all_to_all(jnp.stack([own] * lax.axis_size(axis)), axis, 0, 0)  99 us
    another operation x3, other arithmetic, shards(): jax.scipy.linalg.solve_triangular(lower_factor, cross_terms, lower=True)  83.7 us
    dot_general x1, matrix products, shards(): jnp.einsum('ri,rj->ij', leading, front_local, precision=highest)  55.4 us
    reduce_scatter x1, waiting for transfers between devices, from_root(): own = lax.psum_scatter(padded, axis, scatter_dimension=0, tiled=True)  48 us
    all_to_all x1, waiting for transfers between devices, shards(): lax.all_to_all(packed, 'col', split_axis=0, concat_axis=0, tiled=True)  47.5 us
  transfers between devices with their start and end apart: 12, of which 9 were waited for; matrix products, arithmetic and copies ran while one was open for 2% of the time, Pallas kernels for 0%

profile of v1, /device:TPU:1, one launch (start us, length us, event | category | flops | bytes accessed | tf_op | source)
XLA Modules:
  0.0 1067.5 jit_solution(5512942861937777596)
XLA Ops:
  12.2 46.8 %collective-permute-done.4 = f32[8,256,256]{2,1,0:T(8,128)} collective-permute-done((f32[8,256,256]{2,1,0:T(8,128)}, f32[8,256,256]{2,1,0:T(8,128)}, u32[]{:S(2)}, u32[]{:S(2)}) %collective-permute-start.4) | collective-permute-done | bytes 2097184 | tf_op jit(solution)/shard_map/ppermute | solution.py:16
  62.3 48.4 %collective-permute-done.5 = f32[8,256,256]{2,1,0:T(8,128)} collective-permute-done((f32[8,256,256]{2,1,0:T(8,128)S(1)}, f32[8,256,256]{2,1,0:T(8,128)}, u32[]{:S(2)}, u32[]{:S(2)}) %collective-permute-start.5) | collective-permute-done | bytes 2097184 | tf_op jit(solution)/shard_map/ppermute | solution.py:16
  114.1 44.8 %collective-permute-done.6 = f32[8,256,256]{2,1,0:T(8,128)} collective-permute-done((f32[8,256,256]{2,1,0:T(8,128)S(1)}, f32[8,256,256]{2,1,0:T(8,128)}, u32[]{:S(2)}, u32[]{:S(2)}) %collective-permute-start.6) | collective-permute-done | bytes 2097184 | tf_op jit(solution)/shard_map/ppermute | solution.py:16
  167.2 36.4 %collective-permute-start.2 = (s32[8,2]{0,1:T(2,128)S(1)}, s32[8,2]{0,1:T(2,128)S(1)}, u32[]{:S(2)}, u32[]{:S(2)}) collective-permute-start(s32[8,2]{0,1:T(2,128)S(1)} %broadcast_select_fusion.6), channel_id=1, source_target_pairs={{0,32},{8,40},{16,48},{24,56},{32,64},{40,72},{48,80},{56,88},{64,... | collective-permute-start | bytes 200 | tf_op jit(solution)/shard_map/ppermute | solution.py:16
  211.7 10.0 all-to-all-start.1
  243.7 47.5 %all-to-all-done = f32[8,2,256,256]{3,1,2,0:T(2,128)} async-done(((f32[8,2,256,256]{3,1,2,0:T(2,128)}), f32[8,2,256,256]{3,1,2,0:T(2,128)}, u32[]{:S(2)}, u32[]{:S(2)}) %all-to-all-start) | async-done | bytes 4194336 | tf_op jit(solution)/shard_map/all_to_all | solution.py:78
  312.4 10.4 copy.28
  337.7 48.0 %reduce-scatter.2.cloned.1.call-done = f32[256,1024]{0,1:T(8,128)} async-done(((f32[2048,1024]{0,1:T(8,128)}), f32[256,1024]{0,1:T(8,128)}) %reduce-scatter.2.cloned.1.call-update) | async-done | bytes 1048592 | tf_op jit(solution)/shard_map/reduce_scatter | solution.py:31
  388.4 99.0 %all_to_all.16 = f32[8,256,1024]{2,1,0:T(8,128)S(1)} all-to-all(f32[8,256,1024]{2,1,0:T(8,128)S(1)} %stack.5), channel_id=1, replica_groups=mesh['row'=16,'col'=8] {'col'}, dimensions={0} | all-to-all | bytes 16777216 | tf_op jit(solution)/shard_map/all_to_all | solution.py:33
  487.4 55.4 %fusion.88 = f32[1024,1024]{1,0:T(8,128)} fusion(f32[2048,1024]{1,0:T(8,128)S(1)} %bitcast.144, f32[2048,1024]{0,1:T(8,128)S(1)} %bitcast.142), kind=kOutput, calls=%fused_computation.203 | convolution fusion | flops 25769803776 | bytes 20971520 | tf_op jit(solution)/shard_map/ri,rj->ij/dot_general | solution.py:91
  542.7 29.0 %convolution_bitcast_fusion = f32[1024,1024]{0,1:T(8,128)} fusion(f32[8,256,1024]{2,1,0:T(8,128)S(1)} %all_to_all.16), kind=kOutput, calls=%fused_computation.12 | convolution fusion | flops 25769803776 | bytes 12582912 | tf_op jit(solution)/shard_map/ri,rj->ij/dot_general | solution.py:90
  571.8 141.5 %all-reduce.4.cloned.1.call-done = (f32[1024,1024]{1,0:T(8,128)}, f32[1024,1024]{0,1:T(8,128)}) async-done(((f32[1024,1024]{1,0:T(8,128)}, f32[1024,1024]{0,1:T(8,128)}), (f32[1024,1024]{1,0:T(8,128)}, f32[1024,1024]{0,1:T(8,128)})) %all-reduce.4.cloned.1.call-update) | async-done | bytes 8388624 | tf_op jit(solution)/shard_map/psum | solution.py:92
  725.1 11.7 %cholesky.223 = f32[128,128]{1,0:T(8,128)S(1)} custom-call(f32[128,128]{1,0:T(8,128)S(1)} %cholesky.580), custom_call_target="Cholesky" | custom-call | tf_op jit(solution)/shard_map/jit(cholesky)/cholesky | solution.py:93
  739.4 9.8 custom-call.63
  753.1 11.9 %cholesky.244 = f32[128,128]{1,0:T(8,128)S(1)} custom-call(f32[128,128]{1,0:T(8,128)S(1)} %cholesky.584), custom_call_target="Cholesky" | custom-call | tf_op jit(solution)/shard_map/jit(cholesky)/cholesky | solution.py:93
  778.7 11.7 %cholesky.468 = f32[128,128]{1,0:T(8,128)S(1)} custom-call(f32[128,128]{1,0:T(8,128)S(1)} %cholesky.589), custom_call_target="Cholesky" | custom-call | tf_op jit(solution)/shard_map/jit(cholesky)/cholesky | solution.py:93
  805.0 11.9 %cholesky.487 = f32[128,128]{1,0:T(8,128)S(1)} custom-call(f32[128,128]{1,0:T(8,128)S(1)} %cholesky.594), custom_call_target="Cholesky" | custom-call | tf_op jit(solution)/shard_map/jit(cholesky)/cholesky | solution.py:93
  831.4 11.7 %cholesky.506 = f32[128,128]{1,0:T(8,128)S(1)} custom-call(f32[128,128]{1,0:T(8,128)S(1)} %cholesky.599), custom_call_target="Cholesky" | custom-call | tf_op jit(solution)/shard_map/jit(cholesky)/cholesky | solution.py:93
  844.4 10.2 custom-call.67
  857.9 11.7 %cholesky.526 = f32[128,128]{1,0:T(8,128)S(1)} custom-call(f32[128,128]{1,0:T(8,128)S(1)} %cholesky.604), custom_call_target="Cholesky" | custom-call | tf_op jit(solution)/shard_map/jit(cholesky)/cholesky | solution.py:93
  883.7 11.9 %cholesky.546 = f32[128,128]{1,0:T(8,128)S(1)} custom-call(f32[128,128]{1,0:T(8,128)S(1)} %cholesky.609), custom_call_target="Cholesky" | custom-call | tf_op jit(solution)/shard_map/jit(cholesky)/cholesky | solution.py:93
  909.2 11.7 %cholesky.564 = f32[128,128]{1,0:T(8,128)S(1)} custom-call(f32[128,128]{1,0:T(8,128)S(1)} %convolution_subtract_fusion.11), custom_call_target="Cholesky" | custom-call | tf_op jit(solution)/shard_map/jit(cholesky)/cholesky | solution.py:93
  932.7 22.8 %while.1 = (s32[]{:T(128)}, f32[1024,1024]{1,0:T(8,128)}, s32[8,2]{0,1:T(2,128)S(1)}, f32[8,128,128]{2,1,0:T(8,128)S(1)}, s32[]{:T(128)}) while((s32[]{:T(128)}, f32[1024,1024]{1,0:T(8,128)}, s32[8,2]{0,1:T(2,128)S(1)}, f32[8,128,128]{2,1,0:T(8,128)S(1)}, s32[]{:T(128)}) %tuple.59), condition=%wide.while_cond, body=%wide.while_body.sunk | while | flops 2 | bytes 131181 | solution.py:94
  955.5 78.8 %custom-call.70 = f32[8,128,128]{1,2,0:T(8,128)S(1)} custom-call(f32[8,128,128]{2,1,0:T(8,128)S(1)} %get-tuple-element.12), custom_call_target="InvertDiagBlocksLowerTriangular" | custom-call | tf_op jit(solution)/shard_map/jit(_solve_triangular)/triangular_solve | solution.py:94
  (158 shorter events, 234.8 us)
Async XLA Ops:
  6.5 52.5 %collective-permute-start.4 = (f32[8,256,256]{2,1,0:T(8,128)}, f32[8,256,256]{2,1,0:T(8,128)}, u32[]{:S(2)}, u32[]{:S(2)}) collective-permute-start(f32[8,256,256]{2,1,0:T(8,128)} %param.4), channel_id=1, source_target_pairs={{0,8},{8,16},{16,24},{24,32},{32,40},{40,48},{48,56},{56,64},{64,7... | collective-permute-start | bytes 6291464 | tf_op jit(solution)/shard_map/ppermute | solution.py:16
  60.9 1.3 copy-start.3
  60.9 53.0 %copy-start.5 = (s32[8,2]{0,1:T(2,128)S(1)}, s32[8,2]{0,1:T(2,128)}, u32[]{:S(2)}) copy-start(s32[8,2]{0,1:T(2,128)} %param.5) | copy-start | bytes 196
  61.0 49.7 %collective-permute-start.5 = (f32[8,256,256]{2,1,0:T(8,128)S(1)}, f32[8,256,256]{2,1,0:T(8,128)}, u32[]{:S(2)}, u32[]{:S(2)}) collective-permute-start(f32[8,256,256]{2,1,0:T(8,128)S(1)} %broadcast_select_fusion.1), channel_id=1, source_target_pairs={{0,16},{8,24},{16,32},{24,40},{32,48},{40,56},{48,64},{56,72},{64,... | collective-permute-start | bytes 6291464 | tf_op jit(solution)/shard_map/ppermute | solution.py:16
  112.6 1.5 copy-start.2
  112.6 46.4 %collective-permute-start.6 = (f32[8,256,256]{2,1,0:T(8,128)S(1)}, f32[8,256,256]{2,1,0:T(8,128)}, u32[]{:S(2)}, u32[]{:S(2)}) collective-permute-start(f32[8,256,256]{2,1,0:T(8,128)S(1)} %broadcast_select_fusion.2), channel_id=1, source_target_pairs={{0,32},{8,40},{16,48},{24,56},{32,64},{40,72},{48,80},{56,88},{64,... | collective-permute-start | bytes 6291464 | tf_op jit(solution)/shard_map/ppermute | solution.py:16
  114.0 47.0 %collective-permute-start = (s32[8,2]{0,1:T(2,128)S(1)}, s32[8,2]{0,1:T(2,128)S(1)}, u32[]{:S(2)}, u32[]{:S(2)}) collective-permute-start(s32[8,2]{0,1:T(2,128)S(1)} %pad_add_fusion), channel_id=1, source_target_pairs={{0,8},{8,16},{16,24},{24,32},{32,40},{40,48},{48,56},{56,64},{64,7... | collective-permute-start | bytes 200 | tf_op jit(solution)/shard_map/ppermute | solution.py:16
  160.9 60.8 %collective-permute-start.7 = (f32[8,256,256]{2,1,0:T(8,128)S(1)}, f32[8,256,256]{2,1,0:T(8,128)}, u32[]{:S(2)}, u32[]{:S(2)}) collective-permute-start(f32[8,256,256]{2,1,0:T(8,128)S(1)} %broadcast_select_fusion.3), channel_id=1, source_target_pairs={{0,64},{8,72},{16,80},{24,88},{32,96},{40,104},{48,112},{56,120},{... | collective-permute-start | bytes 6291464 | tf_op jit(solution)/shard_map/ppermute | solution.py:16
  161.0 6.2 collective-permute-start.1
  167.2 39.3 %collective-permute-start.2 = (s32[8,2]{0,1:T(2,128)S(1)}, s32[8,2]{0,1:T(2,128)S(1)}, u32[]{:S(2)}, u32[]{:S(2)}) collective-permute-start(s32[8,2]{0,1:T(2,128)S(1)} %broadcast_select_fusion.6), channel_id=1, source_target_pairs={{0,32},{8,40},{16,48},{24,56},{32,64},{40,72},{48,80},{56,88},{64,... | collective-permute-start | bytes 200 | tf_op jit(solution)/shard_map/ppermute | solution.py:16
  206.6 3.9 collective-permute-start.3
  211.7 25.8 %all-to-all-start.1 = ((s32[8,1,2]{2,1,0:T(1,128)}), s32[8,1,2]{2,1,0:T(1,128)S(1)}, u32[]{:S(2)}, u32[]{:S(2)}) async-start(s32[8,1,2]{2,1,0:T(1,128)} %bitcast.5), calls=%async_computation.1 | async-start | bytes 8192 | tf_op jit(solution)/shard_map/all_to_all | solution.py:79
  237.5 53.7 %all-to-all-start = ((f32[8,2,256,256]{3,1,2,0:T(2,128)}), f32[8,2,256,256]{3,1,2,0:T(2,128)}, u32[]{:S(2)}, u32[]{:S(2)}) async-start(f32[8,2,256,256]{3,1,2,0:T(2,128)} %copy.25), calls=%async_computation | async-start | bytes 8388608 | tf_op jit(solution)/shard_map/all_to_all | solution.py:78
  242.3 143.4 %reduce-scatter.2.cloned.1.call-start = ((), (), s32[]{:S(2)}) async-start(), calls=%async_computation.4 | async-start | bytes 9437184 | tf_op jit(solution)/shard_map/reduce_scatter | solution.py:31
  330.3 3.2 copy-start
  337.6 375.7 %all-reduce.4.cloned.1.call-start = ((), (), s32[]{:S(2)}) async-start(), calls=%async_computation.5 | async-start | bytes 16777216 | tf_op jit(solution)/shard_map/psum | solution.py:92
  387.3 100.1 %slice-start = ((s8[8388608]{0:T(1024)(128)(4,1)}), s8[4194304]{0:T(1024)(128)(4,1)S(1)}, s32[]{:S(2)}) async-start(s8[8388608]{0:T(1024)(128)(4,1)} %bitcast.140), calls=%async_computation.6 | async-start | bytes 8388608
  388.4 99.0 %slice-start.1 = ((s8[8388608]{0:T(1024)(128)(4,1)}), s8[4194304]{0:T(1024)(128)(4,1)S(1)}, s32[]{:S(2)}) async-start(s8[8388608]{0:T(1024)(128)(4,1)} %bitcast.140), calls=%async_computation.7 | async-start | bytes 8388608
  723.1 2.0 copy-start.1
  1034.4 4.3 copy-start.4
Sparse Core Ops, SparseCore 0:
  337.7 47.9 reduce-scatter.1
  571.9 141.3 all-reduce.3
